TPU v7x, 32 devices: a whole 2x2x4 slice. The times are simulated.
32 devices in a mesh: row: 8 (over z, core), col: 2 (over y), head: 2 (over x).
Axes of the slice: x: 2, y: 2, z: 4, core: 2. Of those that a mesh axis runs over, the one named last changes fastest.
Arguments:
- x_lo: float32 [6, 32, 64, 4], P('col', 'row', 'head'), may hold values from -32 to 32
- noise: float32 [6, 32, 64, 16], P('col', 'row'), may hold values from -6 to 6
- t_index: int32 [6], P('col'), may hold values from 0 to 999
- labels: int32 [6], P('col'), may hold values from 0 to 1000
- stale_kv: bfloat16 [2, 6, 16, 32, 1152], P(None, 'col', 'row', None, 'head'), may hold values from -6 to 6
- embed_w: float32 [16, 1152], replicated, may hold values from -1.5 to 1.5
- t_w1: bfloat16 [256, 1152], replicated, may hold values from -0.375 to 0.375
- t_w2: bfloat16 [1152, 1152], P(None, 'row'), may hold values from -0.1875 to 0.1875
- class_table: bfloat16 [1001, 1152], P(None, 'row'), may hold values from -6 to 6
- ada_w: bfloat16 [1152, 6912], P('row'), may hold values from -0.1875 to 0.1875
- qkv_w: bfloat16 [1152, 3, 1152], P(None, None, 'head'), may hold values from -0.1875 to 0.1875
- out_w: bfloat16 [1152, 1152], P('head'), may hold values from -0.1875 to 0.1875
- fc1_w: bfloat16 [1152, 4608], P(None, ('col', 'head')), may hold values from -0.1875 to 0.1875
- fc2_w: bfloat16 [1152, 4608], P(None, ('col', 'head')), may hold values from -0.09375 to 0.09375
Outputs:
- tokens_out: bfloat16 [6, 32, 64, 1152], P('col', 'row', 'head')
All inputs are finite; a program needn't handle non-finite values.
Results may differ from a plain program's by a relative error of at most 0.025.
Values may be sent and summed in bfloat16 or wider, within the bound.
A program may use at most 128 MiB of HBM per device.

v0:
```python
import math
import jax
import jax.numpy as jnp
from jax import lax
from jax.sharding import PartitionSpec as P

HD = 72
TSTEPS = 1000


def padded_2(block, sides, width):
    for axis, dim in sides:
        count = lax.axis_size(axis)
        forward = [(i, i + 1) for i in range(count - 1)]
        backward = [(target, source) for source, target in forward]
        low = lax.ppermute(
            lax.slice_in_dim(block, block.shape[dim] - width, None, axis=dim), axis, forward
        )
        high = lax.ppermute(lax.slice_in_dim(block, 0, width, axis=dim), axis, backward)
        block = jnp.concatenate([low, block, high], axis=dim)
    return block


def upsample_padded(padded):
    upper = padded[:, :-2]
    middle = padded[:, 1:-1]
    lower = padded[:, 2:]
    rows_even = 0.75 * middle + 0.25 * upper
    rows_odd = 0.75 * middle + 0.25 * lower

    def widen(vertical):
        left_side = vertical[:, :, :-2]
        centre = vertical[:, :, 1:-1]
        right_side = vertical[:, :, 2:]
        return jnp.stack(
            [0.75 * centre + 0.25 * left_side, 0.75 * centre + 0.25 * right_side], axis=3
        )

    stacked = jnp.stack([widen(rows_even), widen(rows_odd)], axis=3)
    return stacked.reshape(
        stacked.shape[0], stacked.shape[1], stacked.shape[2], 4 * stacked.shape[-1]
    )


def clamp_edges(padded, axis_dim, at_start, at_end):
    length = padded.shape[axis_dim]
    leading = lax.slice_in_dim(padded, 0, 1, axis=axis_dim)
    second_row = lax.slice_in_dim(padded, 1, 2, axis=axis_dim)
    trailing = lax.slice_in_dim(padded, length - 1, length, axis=axis_dim)
    before_end = lax.slice_in_dim(padded, length - 2, length - 1, axis=axis_dim)
    leading = jnp.where(at_start, second_row, leading)
    trailing = jnp.where(at_end, before_end, trailing)
    return jnp.concatenate(
        [leading, lax.slice_in_dim(padded, 1, length - 1, axis=axis_dim), trailing], axis=axis_dim
    )


def noise_level(t_index):
    step_values = jnp.arange(TSTEPS, dtype=jnp.float32)
    betas = 0.0001 + (0.02 - 0.0001) * step_values / (TSTEPS - 1)
    log_keep = jnp.cumsum(jnp.log(1.0 - betas))
    picked = (jnp.arange(TSTEPS, dtype=jnp.int32)[None, :] == t_index[:, None]).astype(jnp.float32)
    return jnp.exp(jnp.sum(picked * log_keep[None, :], axis=1))


def position_table(row_pos, col_pos, width):
    quarter = width // 4
    omega = 1.0 / 10000.0 ** (jnp.arange(quarter, dtype=jnp.float32) / quarter)
    row_args = row_pos[:, None] * omega[None, :]
    col_args = col_pos[:, None] * omega[None, :]
    row_part = jnp.concatenate([jnp.sin(row_args), jnp.cos(row_args)], axis=1)
    col_part = jnp.concatenate([jnp.sin(col_args), jnp.cos(col_args)], axis=1)
    n_rows = row_pos.shape[0]
    n_cols = col_pos.shape[0]
    return jnp.concatenate(
        [
            jnp.broadcast_to(row_part[:, None, :], (n_rows, n_cols, width // 2)),
            jnp.broadcast_to(col_part[None, :, :], (n_rows, n_cols, width // 2)),
        ],
        axis=2,
    )


def condition(t_index, labels, t_w1, t_w2, class_table):
    half_freq = t_w1.shape[0] // 2
    freqs = jnp.exp(-math.log(10000.0) * jnp.arange(half_freq, dtype=jnp.float32) / half_freq)
    angles = t_index.astype(jnp.float32)[:, None] * freqs[None, :]
    freq_feat = jnp.concatenate([jnp.cos(angles), jnp.sin(angles)], axis=1).astype(jnp.bfloat16)
    t_hidden = jax.nn.silu(jnp.dot(freq_feat, t_w1, preferred_element_type=jnp.float32)).astype(
        jnp.bfloat16
    )
    t_embed = jnp.dot(t_hidden, t_w2, preferred_element_type=jnp.float32)
    onehot = (jnp.arange(class_table.shape[0], dtype=jnp.int32)[None, :] == labels[:, None]).astype(
        jnp.bfloat16
    )
    return t_embed + jnp.dot(onehot, class_table, preferred_element_type=jnp.float32)


def layer_norm(values):
    centre = jnp.mean(values, axis=-1, keepdims=True)
    spread = jnp.mean((values - centre) ** 2, axis=-1, keepdims=True)
    return (values - centre) * lax.rsqrt(spread + 1e-06)


def spread_out(vector):
    return vector[:, None, None, :]


def body(
    x_lo,
    noise,
    t_index,
    labels,
    stale_kv,
    embed_w,
    t_w1,
    t_w2,
    class_table,
    ada_w,
    qkv_w,
    out_w,
    fc1_w,
    fc2_w,
):
    row_index = lax.axis_index("row")
    row_count = lax.axis_size("row")
    head_index = lax.axis_index("head")
    head_count = lax.axis_size("head")
    batch = noise.shape[0]
    tile_rows = noise.shape[1]
    full_cols = noise.shape[2]
    channels = x_lo.shape[3]
    width = embed_w.shape[1]
    abar = noise_level(t_index)
    gathered = lax.all_gather(x_lo, "head", axis=2, tiled=True)
    padded = padded_2(gathered, (("row", 1),), 1)
    padded = clamp_edges(padded, 1, row_index == 0, row_index == row_count - 1)
    padded = jnp.pad(padded, ((0, 0), (0, 0), (1, 1), (0, 0)), mode="edge")
    upsampled = upsample_padded(padded)
    noisy = (
        jnp.sqrt(abar)[:, None, None, None] * upsampled
        + jnp.sqrt(1.0 - abar)[:, None, None, None] * noise
    )
    grouped = noisy.reshape(batch, tile_rows, full_cols, 4, channels)
    total, squares = lax.psum(
        (jnp.sum(grouped, axis=(1, 2, 3)), jnp.sum(grouped * grouped, axis=(1, 2, 3))), "row"
    )
    count = 4.0 * tile_rows * row_count * full_cols
    centre = total / count
    spread = squares / count - centre * centre
    normed = (
        (grouped - centre[:, None, None, None, :])
        * lax.rsqrt(spread + 1e-05)[:, None, None, None, :]
    ).reshape(batch, tile_rows, full_cols, 4 * channels)
    row_pos = (row_index * tile_rows + jnp.arange(tile_rows, dtype=jnp.int32)).astype(jnp.float32)
    col_pos = jnp.arange(full_cols, dtype=jnp.float32)
    pos = position_table(row_pos, col_pos, width)
    tokens = (
        jnp.einsum("bijf,fd->bijd", normed, embed_w, precision=lax.Precision.HIGHEST) + pos[None]
    ).astype(jnp.bfloat16)
    cond_part = condition(t_index, labels, t_w1, t_w2, class_table)
    cond_act = jax.nn.silu(cond_part).astype(jnp.bfloat16)
    modulation = lax.psum(
        jnp.dot(cond_act, ada_w, preferred_element_type=jnp.float32).astype(jnp.bfloat16), "row"
    ).astype(jnp.float32)
    shift1, scale1, gate1, shift2, scale2, gate2 = jnp.split(modulation, 6, axis=1)
    per_image = tile_rows * full_cols
    flat = tokens.astype(jnp.float32)
    normed1 = (layer_norm(flat) * (1.0 + spread_out(scale1)) + spread_out(shift1)).astype(
        jnp.bfloat16
    )
    local_width = qkv_w.shape[2]
    heads_local = local_width // HD
    qkv = jnp.dot(
        normed1.reshape(batch * per_image, width),
        qkv_w.reshape(width, 3 * local_width),
        preferred_element_type=jnp.float32,
    )
    qkv = qkv.astype(jnp.bfloat16).reshape(batch, per_image, 3, heads_local, HD)
    query = qkv[:, :, 0]
    key_local = qkv[:, :, 1]
    value_local = qkv[:, :, 2]
    scale = 1.0 / math.sqrt(HD)
    fresh = (
        jnp.einsum("bqhd,bkhd->bhqk", query, key_local, preferred_element_type=jnp.float32) * scale
    )
    top_start = jnp.max(fresh, axis=-1)
    probs = jnp.exp(fresh - top_start[..., None])
    mass_start = jnp.sum(probs, axis=-1)
    acc_start = jnp.einsum(
        "bhqk,bkhd->bhqd",
        probs.astype(jnp.bfloat16),
        value_local,
        preferred_element_type=jnp.float32,
    )
    stale_local = stale_kv.reshape(2, batch, -1, local_width)
    per_device = stale_local.shape[2]
    piece = lax.all_gather(stale_local, "row", axis=2, tiled=True)
    key_count = piece.shape[2]
    coarse_key = piece[0].reshape(batch, key_count, heads_local, HD)
    coarse_value = piece[1].reshape(batch, key_count, heads_local, HD)
    scores = jnp.einsum(
        "bqhd,bkhd->bhqk", query, coarse_key, preferred_element_type=jnp.float32
    ) * scale + math.log(4.0)
    key_device = jnp.arange(key_count, dtype=jnp.int32) // per_device
    scores = jnp.where((key_device == row_index)[None, None, None, :], jnp.float32(-1e30), scores)
    new_top = jnp.maximum(top_start, jnp.max(scores, axis=-1))
    shrink = jnp.exp(top_start - new_top)
    weights = jnp.exp(scores - new_top[..., None])
    new_mass = mass_start * shrink + jnp.sum(weights, axis=-1)
    new_acc = acc_start * shrink[..., None] + jnp.einsum(
        "bhqk,bkhd->bhqd",
        weights.astype(jnp.bfloat16),
        coarse_value,
        preferred_element_type=jnp.float32,
    )
    attended = (new_acc / new_mass[..., None]).astype(jnp.bfloat16)
    attended = attended.transpose(0, 2, 1, 3).reshape(batch * per_image, local_width)
    attn_part = jnp.dot(attended, out_w, preferred_element_type=jnp.float32).reshape(
        batch, tile_rows, full_cols, width
    )
    half_cols = full_cols // head_count
    col_start = head_index * half_cols
    projected = lax.psum(attn_part.astype(jnp.bfloat16), "head").astype(jnp.float32)
    mid = (flat + spread_out(gate1) * projected).astype(jnp.bfloat16)
    normed2 = (
        layer_norm(mid.astype(jnp.float32)) * (1.0 + spread_out(scale2)) + spread_out(shift2)
    ).astype(jnp.bfloat16)
    mid_half = lax.dynamic_slice_in_dim(mid, col_start, half_cols, 2)
    normed2_rows = normed2.reshape(batch * per_image, width)
    up_piece = lax.all_gather(fc1_w, "col", axis=1, tiled=True)
    down_piece = lax.all_gather(fc2_w, "col", axis=1, tiled=True)
    hidden = jax.nn.gelu(
        jnp.dot(normed2_rows, up_piece, preferred_element_type=jnp.float32), approximate=True
    ).astype(jnp.bfloat16)
    mlp_part = lax.dot_general(
        hidden, down_piece, (((1,), (1,)), ((), ())), preferred_element_type=jnp.float32
    )
    mlp_term = lax.psum_scatter(
        mlp_part.reshape(batch, tile_rows, full_cols, width).astype(jnp.bfloat16),
        "head",
        scatter_dimension=2,
        tiled=True,
    ).astype(jnp.float32)
    tokens_out = (mid_half.astype(jnp.float32) + spread_out(gate2) * mlp_term).astype(jnp.bfloat16)
    return tokens_out


def solution(mesh):
    placed = (
        P("col", "row", "head", None),
        P("col", "row", None, None),
        P("col"),
        P("col"),
        P(None, "col", "row", None, "head"),
        P(),
        P(),
        P(None, "row"),
        P(None, "row"),
        P("row", None),
        P(None, None, "head"),
        P("head", None),
        P(None, ("col", "head")),
        P(None, ("col", "head")),
    )
    return jax.shard_map(
        body, mesh=mesh, in_specs=placed, out_specs=P("col", "row", "head", None), check_vma=False
    )
```

profile of v0, /device:TPU:0, one launch (start us, length us, event | category | flops | bytes accessed | tf_op | source)
XLA Modules:
  0.0 356.1 jit_solution(11685589510042785841)
XLA Ops:
  7.4 1.0 copy.66
  8.5 8.5 %all_gather.12 = f32[3,4,64,4]{3,1,0,2:T(4,128)S(1)} all-gather(f32[3,4,32,4]{3,1,0,2:T(4,128)S(1)} %copy.66), channel_id=1, replica_groups=mesh['row'=8,'col'=2,'head'=2] {'head'}, dimensions={2}, use_global_device_ids=true | all-gather | bytes 18432 | tf_op jit(solution)/shard_map/all_gather | solution.py:135
  17.0 0.7 copy-done.4
  17.7 0.8 fusion.105
  18.6 1.3 collective-permute-start
  19.9 1.3 collective-permute-start.1
  21.2 2.3 copy.80
  23.6 0.7 convert_element_type.83
  24.4 1.5 fusion.66
  25.9 0.7 convolution_convert_fusion
  26.6 33.9 %psum.30 = bf16[3,6912]{1,0:T(4,128)(2,1)S(1)} all-reduce(bf16[3,6912]{1,0:T(4,128)(2,1)S(1)} %convolution_convert_fusion), channel_id=1, replica_groups=mesh['row'=8,'col'=2,'head'=2] {'row'}, use_global_device_ids=true, to_apply=%region_9.10 | all-reduce | flops 20736 | bytes 82944 | tf_op jit(solution)/shard_map/psum | solution.py:163
  60.6 0.6 fusion.106
  61.2 0.3 reduce-window.9
  61.8 0.2 select_reduce_fusion
  62.0 0.4 fusion.48
  62.8 0.2 pad_maximum_fusion
  63.2 0.2 broadcast_select_fusion.1
  64.6 14.1 %all-reduce.1 = (f32[3,4]{1,0:T(4,128)S(1)}, f32[3,4]{1,0:T(4,128)S(1)}) all-reduce(f32[3,4]{1,0:T(4,128)S(1)} %reduce_sum.105, f32[3,4]{1,0:T(4,128)S(1)} %reduce_sum.102), channel_id=1, replica_groups=mesh['row'=8,'col'=2,'head'=2] {'row'}, use_global_device_ids=true, to_apply=%region_8.9 | all-reduce | flops 24 | bytes 192 | tf_op jit(solution)/shard_map/psum | solution.py:145
  78.8 4.5 %convert_reduce_fusion = (f32[3,4,64]{2,1,0:T(4,128)S(1)}, bf16[3,4,64,1152]{3,2,1,0:T(8,128)(2,1)S(1)}) fusion(f32[4,64,1152]{2,1,0:T(8,128)S(1)} %pad_maximum_fusion, f32[16,1152]{1,0:T(8,128)} %param.19, f32[3,4,64,16]{2,3,1,0:T(8,128)S(1)} %get-tuple-element.13, f32[3,16]{1,0:T(4,128)S(1)} %mul.254, f32[3,16]{1,0:T(4,128)S(1)} %sub.91), kind=kOutput, calls=%fused_computation.21 | convolution fusion | flops 173432064 | bytes 3075456 | tf_op jit(solution)/shard_map/bijf,fd->bijd/dot_general | solution.py:159
  83.4 0.6 fusion.20
  84.0 1.3 fusion.23
  85.3 5.0 %convolution_convert_fusion.2 = bf16[768,1728]{0,1:T(8,128)(2,1)} fusion(bf16[768,1152]{1,0:T(8,128)(2,1)S(1)} %bitcast.108, bf16[1152,1728]{0,1:T(8,128)(2,1)S(1)} %bitcast.112), kind=kOutput, calls=%fused_computation.44 | convolution fusion | flops 3058974720 | bytes 8404992 | tf_op jit(solution)/shard_map/dot_general | solution.py:174
  90.3 6.9 %reshape.150 = bf16[3,256,3,8,72]{1,0,4,3,2:T(4,128)(2,1)} reshape(bf16[768,1728]{0,1:T(8,128)(2,1)} %convolution_convert_fusion.2) | data formatting | bytes 5308416 | tf_op jit(solution)/shard_map/reshape | solution.py:179
  97.2 3.3 fusion.104
  100.5 1.1 multiply_reduce_fusion
  101.6 1.1 fusion.14
  102.7 2.3 fusion.35
  105.0 9.4 %fusion.103 = (bf16[1,3,512,576]{3,0,1,2:T(2,128)(2,1)}, bf16[1,3,512,576]{3,0,1,2:T(2,128)(2,1)}) fusion(bf16[2,3,512,576]{3,0,1,2:T(2,128)(2,1)} %all-gather.4.cloned.1.call-done), kind=kLoop, calls=%fused_computation.162 | loop fusion | bytes 7077888 | tf_op jit(solution)/shard_map/slice | solution.py:200
  114.5 8.5 %copy.81 = bf16[1,3,512,576]{2,3,1,0:T(8,128)(2,1)} copy(bf16[1,3,512,576]{3,0,1,2:T(2,128)(2,1)} %get-tuple-element.14) | data formatting | bytes 3538944 | tf_op jit(solution)/shard_map/slice | solution.py:200
  123.0 7.8 %fusion.2 = (f32[3,8,256]{2,1,0:T(8,128)S(1)}, f32[3,8,256,512]{3,2,1,0:T(8,128)}) fusion(pred[512]{0:T(512)(128)(4,1)S(1)} %fusion.73, bf16[3,512,8,72]{1,3,2,0:T(8,128)(2,1)} %bitcast.109, bf16[3,256,1,8,72]{1,0,4,3,2:T(4,128)(2,1)S(1)} %get-tuple-element.18), kind=kOutput, calls=%fused_computation.5 | convolution fusion | flops 465561600 | bytes 15262208 | tf_op jit(solution)/shard_map/bqhd,bkhd->bhqk/dot_general | solution.py:202
  130.8 8.5 %copy.82 = bf16[1,3,512,576]{2,3,1,0:T(8,128)(2,1)} copy(bf16[1,3,512,576]{3,0,1,2:T(2,128)(2,1)} %get-tuple-element.15) | data formatting | bytes 3538944 | tf_op jit(solution)/shard_map/slice | solution.py:201
  139.3 8.3 %fusion = f32[3,8,256]{2,1,0:T(8,128)S(1)} fusion(f32[3,8,256,512]{3,2,1,0:T(8,128)} %get-tuple-element.52, f32[3,8,256]{2,1,0:T(8,128)S(1)} %max.18, pred[512]{0:T(512)(128)(4,1)S(1)} %fusion.73), kind=kLoop, calls=%fused_computation.2 | loop fusion | flops 15722496 | bytes 12632576 | tf_op jit(solution)/shard_map/reduce_sum | solution.py:210
  147.6 6.1 %fusion.41 = bf16[3,256,8,72]{1,3,2,0:T(8,128)(2,1)} fusion(f32[3,8,256,72]{2,3,1,0:T(8,128)} %fusion.35, bf16[3,512,8,72]{1,3,2,0:T(8,128)(2,1)} %bitcast.106, f32[3,8,256,512]{3,2,1,0:T(8,128)S(1)} %copy-done.3, f32[3,8,256]{2,1,0:T(8,128)S(1)} %max.18, pred[512]{0:T(512)(128)(4,1)S(1)} %fusion.73, f32[3,256,8]{1,2,0:T(8,128)S(1)} %get-tuple-element.11, ...), kind=kOutput, calls=%fused_computation.51 | convolution fusion | flops 470482944 | bytes 17080832 | tf_op jit(solution)/shard_map/bhqk,bkhd->bhqd/dot_general | solution.py:211
  153.8 4.0 %reshape.155 = bf16[3,4,64,576]{2,1,3,0:T(4,128)(2,1)} reshape(bf16[3,256,8,72]{1,3,2,0:T(8,128)(2,1)} %fusion.41) | data formatting | bytes 1769472 | tf_op jit(solution)/shard_map/dot_general | solution.py:219
  157.8 4.5 %convolution_convert_fusion.1 = bf16[3,4,64,1152]{3,2,1,0:T(8,128)(2,1)} fusion(bf16[3,4,64,576]{2,1,3,0:T(4,128)(2,1)} %reshape.155, bf16[576,1152]{1,0:T(8,128)(2,1)S(1)} %copy-done.6), kind=kOutput, calls=%fused_computation.43 | convolution fusion | flops 1020100608 | bytes 3981312 | tf_op jit(solution)/shard_map/dot_general | solution.py:219
  162.4 0.5 all-gather.6.cloned.1.call-update
  163.0 0.5 all-gather.8.cloned.1.call-update
  163.5 0.3 reduce-scatter.2.cloned.1.call-start
  163.8 52.8 %all-reduce.4.cloned.1.call-done = bf16[3,4,64,1152]{3,2,1,0:T(8,128)(2,1)} async-done(((bf16[3,4,64,1152]{3,2,1,0:T(8,128)(2,1)}), bf16[3,4,64,1152]{3,2,1,0:T(8,128)(2,1)}) %all-reduce.4.cloned.1.call-update) | async-done | bytes 1769488 | tf_op jit(solution)/shard_map/psum | solution.py:224
  216.6 2.2 convert_reduce_fusion.1
  218.8 0.6 fusion.24
  219.4 0.6 copy-done.2
  220.0 2.5 fusion.27
  222.5 9.3 %all-gather.6.cloned.1.call-done = bf16[1152,2304]{1,0:T(8,128)(2,1)} async-done(((bf16[1152,1152]{1,0:T(8,128)(2,1)}), bf16[1152,2304]{1,0:T(8,128)(2,1)}) %all-gather.6.cloned.1.call-update) | async-done | bytes 5308432 | tf_op jit(solution)/shard_map/all_gather | solution.py:231
  231.8 70.6 %all-gather.8.cloned.1.call-done = bf16[1152,2304]{1,0:T(8,128)(2,1)} async-done(((bf16[1152,1152]{1,0:T(8,128)(2,1)}), bf16[1152,2304]{1,0:T(8,128)(2,1)}) %all-gather.8.cloned.1.call-update) | async-done | bytes 5308432 | tf_op jit(solution)/shard_map/all_gather | solution.py:232
  302.4 15.5 %fusion.31 = bf16[768,1152]{1,0:T(8,128)(2,1)} fusion(bf16[1152,2304]{1,0:T(8,128)(2,1)} %all-gather.8.cloned.1.call-done, bf16[768,1152]{1,0:T(8,128)(2,1)} %bitcast.107, bf16[1152,2304]{1,0:T(8,128)(2,1)} %all-gather.6.cloned.1.call-done), kind=kOutput, calls=%fused_computation.41 | convolution fusion | flops 8170536960 | bytes 14155776 | tf_op jit(solution)/shard_map/dot_general | solution.py:236
  317.9 28.5 %reduce-scatter.2.cloned.1.call-done = bf16[3,4,32,1152]{3,2,1,0:T(8,128)(2,1)} async-done(((bf16[3,4,64,1152]{3,2,1,0:T(8,128)(2,1)}), bf16[3,4,32,1152]{3,2,1,0:T(8,128)(2,1)}) %reduce-scatter.2.cloned.1.call-update) | async-done | bytes 884752 | tf_op jit(solution)/shard_map/reduce_scatter | solution.py:239
  346.4 2.6 add_convert_fusion
  (80 shorter events, 2.6 us)
Async XLA Ops:
  7.4 18.5 %copy-start = (bf16[144,6912]{1,0:T(8,128)(2,1)S(1)}, bf16[144,6912]{1,0:T(8,128)(2,1)}, u32[]{:S(2)}) copy-start(bf16[144,6912]{1,0:T(8,128)(2,1)} %param.23) | copy-start | bytes 5971972
  7.4 54.4 %copy-start.11 = (s32[3]{0:T(128)S(1)}, s32[3]{0:T(128)}, u32[]{:S(2)}) copy-start(s32[3]{0:T(128)} %param.16) | copy-start | bytes 40
  7.4 18.5 %copy-start.10 = (s32[3]{0:T(128)S(1)}, s32[3]{0:T(128)}, u32[]{:S(2)}) copy-start(s32[3]{0:T(128)} %param.17) | copy-start | bytes 40
  7.4 18.5 %copy-start.7 = (bf16[1001,144]{0,1:T(8,128)(2,1)S(1)}, bf16[1001,144]{0,1:T(8,128)(2,1)}, u32[]{:S(2)}) copy-start(bf16[1001,144]{0,1:T(8,128)(2,1)} %param.22) | copy-start | bytes 864868
  7.4 97.6 %all-gather.4.cloned.1.call-start = ((), (), s32[]{:S(2)}) async-start(), calls=%async_computation.1 | async-start | bytes 4423680 | tf_op jit(solution)/shard_map/all_gather | solution.py:198
  17.0 0.7 copy-start.4
  18.6 44.7 %collective-permute-start = (f32[3,1,64,4]{3,1,0,2:T(1,128)}, f32[3,1,64,4]{3,1,0,2:T(1,128)S(1)}, u32[]{:S(2)}, u32[]{:S(2)}) collective-permute-start(f32[3,1,64,4]{3,1,0,2:T(1,128)} %get-tuple-element.21), channel_id=1, source_target_pairs={{0,4},{4,8},{8,12},{12,16},{16,20},{20,24},{24,28},{1,5},{5,9},{9,... | collective-permute-start | bytes 9224 | tf_op jit(solution)/shard_map/ppermute | solution.py:16
  19.9 43.4 %collective-permute-start.1 = (f32[3,1,64,4]{3,1,0,2:T(1,128)}, f32[3,1,64,4]{3,1,0,2:T(1,128)S(1)}, u32[]{:S(2)}, u32[]{:S(2)}) collective-permute-start(f32[3,1,64,4]{3,1,0,2:T(1,128)} %get-tuple-element.22), channel_id=1, source_target_pairs={{4,0},{8,4},{12,8},{16,12},{20,16},{24,20},{28,24},{5,1},{9,5},{13... | collective-permute-start | bytes 9224 | tf_op jit(solution)/shard_map/ppermute | solution.py:19
  23.5 193.1 %all-reduce.4.cloned.1.call-start = ((), (), s32[]{:S(2)}) async-start(), calls=%async_computation.2 | async-start | bytes 3538944 | tf_op jit(solution)/shard_map/psum | solution.py:224
  26.6 36.4 %copy-start.5 = (f32[3,4,64,4]{3,1,0,2:T(4,128)S(1)}, f32[3,4,64,4]{3,1,0,2:T(4,128)}, u32[]{:S(2)}) copy-start(f32[3,4,64,4]{3,1,0,2:T(4,128)} %copy-done.4) | copy-start | bytes 36868
  61.5 2.7 copy-start.8
  78.8 6.5 %copy-start.12 = (bf16[1152,3,576]{0,2,1:T(8,128)(2,1)S(1)}, bf16[1152,3,576]{0,2,1:T(8,128)(2,1)}, u32[]{:S(2)}) copy-start(bf16[1152,3,576]{0,2,1:T(8,128)(2,1)} %param.24) | copy-start | bytes 11943940
  139.3 8.4 %copy-start.3 = (f32[3,8,256,512]{3,2,1,0:T(8,128)S(1)}, f32[3,8,256,512]{3,2,1,0:T(8,128)}, u32[]{:S(2)}) copy-start(f32[3,8,256,512]{3,2,1,0:T(8,128)} %get-tuple-element.52) | copy-start | bytes 37748740
  153.8 4.0 %copy-start.6 = (bf16[576,1152]{1,0:T(8,128)(2,1)S(1)}, bf16[576,1152]{1,0:T(8,128)(2,1)}, u32[]{:S(2)}) copy-start(bf16[576,1152]{1,0:T(8,128)(2,1)} %param.25) | copy-start | bytes 3981316
  162.3 54.3 %copy-start.9 = (f32[3,1152]{1,0:T(4,128)S(1)}, f32[3,1152]{1,0:T(4,128)}, u32[]{:S(2)}) copy-start(f32[3,1152]{1,0:T(4,128)} %get-tuple-element.27) | copy-start | bytes 41476
  162.3 69.5 %all-gather.6.cloned.1.call-start = ((), (), s32[]{:S(2)}) async-start(), calls=%async_computation.3 | async-start | bytes 7962624 | tf_op jit(solution)/shard_map/all_gather | solution.py:231
  162.9 139.5 %all-gather.8.cloned.1.call-start = ((), (), s32[]{:S(2)}) async-start(), calls=%async_computation.4 | async-start | bytes 7962624 | tf_op jit(solution)/shard_map/all_gather | solution.py:232
  163.5 182.9 %reduce-scatter.2.cloned.1.call-start = ((), (), s32[]{:S(2)}) async-start(), calls=%async_computation.5 | async-start | bytes 2654208 | tf_op jit(solution)/shard_map/reduce_scatter | solution.py:239
  218.8 1.2 copy-start.2
  302.4 46.6 %copy-start.1 = (bf16[144,6912]{1,0:T(8,128)(2,1)S(1)}, bf16[144,6912]{1,0:T(8,128)(2,1)}, u32[]{:S(2)}) copy-start(bf16[144,6912]{1,0:T(8,128)(2,1)} %param.23) | copy-start | bytes 5971972
Sparse Core Ops, SparseCore 0:
  23.6 50.2 all-gather.3
  162.4 54.0 all-reduce.3
  318.0 28.3 reduce-scatter.1
Sparse Core Ops, SparseCore 1:
  164.4 67.4 all-gather.5
  233.2 69.1 all-gather.7
where the time goes:
time: 357 us; the launch traced here: 356 us
  waiting for transfers between devices  162 us (45%)
  blocking collectives  56.5 us (16%)
  matrix products  49 us (14%)
  local copies, waits for them, and re-layouts  47.9 us (13%)
  other arithmetic  22.4 us (6%)
  between operations  14.9 us (4%)
    all_gather x1, waiting for transfers between devices, body(): down_piece = lax.all_gather(fc2_w, 'col', axis=1, tiled=True)  70.6 us
    psum x1, waiting for transfers between devices, body(): lax.psum(attn_part.astype(jnp.bfloat16), 'head').astype(jnp.float32)  52.8 us
    psum x1, blocking collectives, body(): lax.psum(jnp.dot(cond_act, ada_w, preferred_element_type=jnp.float32).ast...  33.9 us
    reduce_scatter x1, waiting for transfers between devices, body(): lax.psum_scatter(mlp_part.reshape(batch, tile_rows, full_cols, width).ast...  28.5 us
    slice x2, local copies, waits for them, and re-layouts, body(): coarse_key = piece[0].reshape(batch, key_count, heads_local, HD)  17.9 us
    dot_general x1, matrix products, body(): lax.dot_general(hidden, down_piece, (((1,), (1,)), ((), ())), preferred_e...  15.5 us
    psum x1, blocking collectives, body(): lax.psum((jnp.sum(grouped, axis=(1, 2, 3)), jnp.sum(grouped * grouped, ax...  14.1 us
    all_gather x1, waiting for transfers between devices, body(): up_piece = lax.all_gather(fc1_w, 'col', axis=1, tiled=True)  9.34 us
  transfers between devices with their start and end apart: 7, of which 4 were waited for; matrix products, arithmetic and copies ran while one was open for 11% of the time, Pallas kernels for 0%

commit v1 on v0

--- a/solution.py
+++ b/solution.py
@@ -221,7 +221,9 @@
     )
     half_cols = full_cols // head_count
     col_start = head_index * half_cols
-    projected = lax.psum(attn_part.astype(jnp.bfloat16), "head").astype(jnp.float32)
+    projected = jnp.sum(lax.all_gather(attn_part.astype(jnp.bfloat16), "head"), axis=0).astype(
+        jnp.float32
+    )
     mid = (flat + spread_out(gate1) * projected).astype(jnp.bfloat16)
     normed2 = (
         layer_norm(mid.astype(jnp.float32)) * (1.0 + spread_out(scale2)) + spread_out(shift2)

time: 357 us -> 405 us (1.13)
  waiting for transfers between devices: 162 us -> 207 us
  other arithmetic: 22.4 us -> 26.8 us
    all_gather x1, waiting for transfers between devices: 9.34 us -> 70.7 us  [body(): up_piece = lax.all_gather(fc1_w, 'col', axis=1, tiled=True)]
    psum x1 -> x0, waiting for transfers between devices: 52.8 us -> none  [body(): lax.psum(attn_part.astype(jnp.bfloat16), 'head').astype(jnp.float32)]
    all_gather x0 -> x1, waiting for transfers between devices: none -> 46.1 us  [body(): lax.all_gather(attn_part.astype(jnp.bfloat16), 'head')]
    all_gather x1, waiting for transfers between devices: 70.6 us -> 60.6 us  [body(): down_piece = lax.all_gather(fc2_w, 'col', axis=1, tiled=True)]
    reduce_sum x0 -> x1, other arithmetic: none -> 4.35 us  [body(): jnp.sum(lax.all_gather(attn_part.astype(jnp.bfloat16), 'head'), axis=0)]
where the time goes in v1:
time: 405 us; the launch traced here: 404 us
  waiting for transfers between devices  207 us (51%)
  blocking collectives  56.5 us (14%)
  matrix products  48.9 us (12%)
  local copies, waits for them, and re-layouts  47.9 us (12%)
  other arithmetic  26.8 us (7%)
  between operations  13.5 us (3%)
    all_gather x1, waiting for transfers between devices, body(): up_piece = lax.all_gather(fc1_w, 'col', axis=1, tiled=True)  70.7 us
    all_gather x1, waiting for transfers between devices, body(): down_piece = lax.all_gather(fc2_w, 'col', axis=1, tiled=True)  60.6 us
    all_gather x1, waiting for transfers between devices, body(): lax.all_gather(attn_part.astype(jnp.bfloat16), 'head')  46.1 us
    psum x1, blocking collectives, body(): lax.psum(jnp.dot(cond_act, ada_w, preferred_element_type=jnp.float32).ast...  33.9 us
    reduce_scatter x1, waiting for transfers between devices, body(): lax.psum_scatter(mlp_part.reshape(batch, tile_rows, full_cols, width).ast...  28.5 us
    slice x2, local copies, waits for them, and re-layouts, body(): coarse_key = piece[0].reshape(batch, key_count, heads_local, HD)  17.9 us
    dot_general x1, matrix products, body(): lax.dot_general(hidden, down_piece, (((1,), (1,)), ((), ())), preferred_e...  15.5 us
    psum x1, blocking collectives, body(): lax.psum((jnp.sum(grouped, axis=(1, 2, 3)), jnp.sum(grouped * grouped, ax...  14.1 us
  transfers between devices with their start and end apart: 7, of which 4 were waited for; matrix products, arithmetic and copies ran while one was open for 11% of the time, Pallas kernels for 0%

profile of v1, /device:TPU:0, one launch (start us, length us, event | category | flops | bytes accessed | tf_op | source)
XLA Modules:
  0.0 403.9 jit_solution(1836817710751549239)
XLA Ops:
  6.6 1.0 copy.66
  7.6 8.5 %all_gather.18 = f32[3,4,64,4]{3,1,0,2:T(4,128)S(1)} all-gather(f32[3,4,32,4]{3,1,0,2:T(4,128)S(1)} %copy.66), channel_id=1, replica_groups=mesh['row'=8,'col'=2,'head'=2] {'head'}, dimensions={2}, use_global_device_ids=true | all-gather | bytes 18432 | tf_op jit(solution)/shard_map/all_gather | solution.py:135
  16.2 0.7 copy-done.4
  16.9 0.8 fusion.105
  17.7 1.3 collective-permute-start
  19.0 1.3 collective-permute-start.1
  20.3 2.3 copy.80
  22.8 0.7 convert_element_type.85
  23.5 1.5 fusion.66
  25.1 0.7 convolution_convert_fusion
  25.8 33.9 %psum.23 = bf16[3,6912]{1,0:T(4,128)(2,1)S(1)} all-reduce(bf16[3,6912]{1,0:T(4,128)(2,1)S(1)} %convolution_convert_fusion), channel_id=1, replica_groups=mesh['row'=8,'col'=2,'head'=2] {'row'}, use_global_device_ids=true, to_apply=%region_9.10 | all-reduce | flops 20736 | bytes 82944 | tf_op jit(solution)/shard_map/psum | solution.py:163
  59.7 0.6 fusion.106
  60.4 0.3 reduce-window.9
  61.2 0.4 fusion.48
  61.9 0.2 pad_maximum_fusion
  62.4 0.2 broadcast_select_fusion.1
  63.7 14.1 %all-reduce.1 = (f32[3,4]{1,0:T(4,128)S(1)}, f32[3,4]{1,0:T(4,128)S(1)}) all-reduce(f32[3,4]{1,0:T(4,128)S(1)} %reduce_sum.117, f32[3,4]{1,0:T(4,128)S(1)} %reduce_sum.114), channel_id=1, replica_groups=mesh['row'=8,'col'=2,'head'=2] {'row'}, use_global_device_ids=true, to_apply=%region_8.9 | all-reduce | flops 24 | bytes 192 | tf_op jit(solution)/shard_map/psum | solution.py:145
  78.0 4.5 %convert_reduce_fusion = (f32[3,4,64]{2,1,0:T(4,128)S(1)}, bf16[3,4,64,1152]{3,2,1,0:T(8,128)(2,1)S(1)}) fusion(f32[4,64,1152]{2,1,0:T(8,128)S(1)} %pad_maximum_fusion, f32[16,1152]{1,0:T(8,128)} %param.19, f32[3,4,64,16]{2,3,1,0:T(8,128)S(1)} %get-tuple-element.13, f32[3,16]{1,0:T(4,128)S(1)} %mul.254, f32[3,16]{1,0:T(4,128)S(1)} %sub.91), kind=kOutput, calls=%fused_computation.21 | convolution fusion | flops 173432064 | bytes 3075456 | tf_op jit(solution)/shard_map/bijf,fd->bijd/dot_general | solution.py:159
  82.6 0.6 fusion.20
  83.2 1.3 fusion.23
  84.5 5.0 %convolution_convert_fusion.2 = bf16[768,1728]{0,1:T(8,128)(2,1)} fusion(bf16[768,1152]{1,0:T(8,128)(2,1)S(1)} %bitcast.110, bf16[1152,1728]{0,1:T(8,128)(2,1)S(1)} %bitcast.114), kind=kOutput, calls=%fused_computation.44 | convolution fusion | flops 3058974720 | bytes 8404992 | tf_op jit(solution)/shard_map/dot_general | solution.py:174
  89.5 6.9 %reshape.150 = bf16[3,256,3,8,72]{1,0,4,3,2:T(4,128)(2,1)} reshape(bf16[768,1728]{0,1:T(8,128)(2,1)} %convolution_convert_fusion.2) | data formatting | bytes 5308416 | tf_op jit(solution)/shard_map/reshape | solution.py:179
  96.4 3.3 fusion.104
  99.7 1.0 multiply_reduce_fusion
  100.7 1.1 fusion.14
  101.8 2.3 fusion.35
  104.2 9.4 %fusion.103 = (bf16[1,3,512,576]{3,0,1,2:T(2,128)(2,1)}, bf16[1,3,512,576]{3,0,1,2:T(2,128)(2,1)}) fusion(bf16[2,3,512,576]{3,0,1,2:T(2,128)(2,1)} %all-gather.6.cloned.1.call-done), kind=kLoop, calls=%fused_computation.162 | loop fusion | bytes 7077888 | tf_op jit(solution)/shard_map/slice | solution.py:200
  113.6 8.5 %copy.81 = bf16[1,3,512,576]{2,3,1,0:T(8,128)(2,1)} copy(bf16[1,3,512,576]{3,0,1,2:T(2,128)(2,1)} %get-tuple-element.14) | data formatting | bytes 3538944 | tf_op jit(solution)/shard_map/slice | solution.py:200
  122.1 7.8 %fusion.2 = (f32[3,8,256]{2,1,0:T(8,128)S(1)}, f32[3,8,256,512]{3,2,1,0:T(8,128)}) fusion(pred[512]{0:T(512)(128)(4,1)S(1)} %fusion.73, bf16[3,512,8,72]{1,3,2,0:T(8,128)(2,1)} %bitcast.111, bf16[3,256,1,8,72]{1,0,4,3,2:T(4,128)(2,1)S(1)} %get-tuple-element.18), kind=kOutput, calls=%fused_computation.5 | convolution fusion | flops 465561600 | bytes 15262208 | tf_op jit(solution)/shard_map/bqhd,bkhd->bhqk/dot_general | solution.py:202
  129.9 8.5 %copy.82 = bf16[1,3,512,576]{2,3,1,0:T(8,128)(2,1)} copy(bf16[1,3,512,576]{3,0,1,2:T(2,128)(2,1)} %get-tuple-element.15) | data formatting | bytes 3538944 | tf_op jit(solution)/shard_map/slice | solution.py:201
  138.4 8.3 %fusion = f32[3,8,256]{2,1,0:T(8,128)S(1)} fusion(f32[3,8,256,512]{3,2,1,0:T(8,128)} %get-tuple-element.52, f32[3,8,256]{2,1,0:T(8,128)S(1)} %max.18, pred[512]{0:T(512)(128)(4,1)S(1)} %fusion.73), kind=kLoop, calls=%fused_computation.2 | loop fusion | flops 15722496 | bytes 12632576 | tf_op jit(solution)/shard_map/reduce_sum | solution.py:210
  146.8 6.1 %fusion.41 = bf16[3,256,8,72]{1,3,2,0:T(8,128)(2,1)} fusion(f32[3,8,256,72]{2,3,1,0:T(8,128)} %fusion.35, bf16[3,512,8,72]{1,3,2,0:T(8,128)(2,1)} %bitcast.108, f32[3,8,256,512]{3,2,1,0:T(8,128)S(1)} %copy-done.3, f32[3,8,256]{2,1,0:T(8,128)S(1)} %max.18, pred[512]{0:T(512)(128)(4,1)S(1)} %fusion.73, f32[3,256,8]{1,2,0:T(8,128)S(1)} %get-tuple-element.11, ...), kind=kOutput, calls=%fused_computation.51 | convolution fusion | flops 470482944 | bytes 17080832 | tf_op jit(solution)/shard_map/bhqk,bkhd->bhqd/dot_general | solution.py:211
  152.9 4.0 reshape.156
  156.9 4.4 %convolution_convert_fusion.1 = bf16[3,4,64,1152]{3,2,1,0:T(8,128)(2,1)} fusion(bf16[3,4,64,576]{2,1,3,0:T(4,128)(2,1)} %reshape.156, bf16[576,1152]{1,0:T(8,128)(2,1)S(1)} %copy-done.6), kind=kOutput, calls=%fused_computation.43 | convolution fusion | flops 1020100608 | bytes 3981312 | tf_op jit(solution)/shard_map/dot_general | solution.py:219
  161.5 0.7 all-gather.10.cloned.1.call-update
  162.2 0.5 all-gather.8.cloned.1.call-update
  162.7 0.3 reduce-scatter.2.cloned.1.call-start
  163.0 46.1 %all-gather.12.cloned.1.call-done = bf16[6,4,64,1152]{3,2,1,0:T(8,128)(2,1)} async-done(((bf16[3,4,64,1152]{3,2,1,0:T(8,128)(2,1)}), bf16[6,4,64,1152]{3,2,1,0:T(8,128)(2,1)}) %all-gather.12.cloned.1.call-update) | async-done | bytes 3538960 | tf_op jit(solution)/shard_map/all_gather | solution.py:224
  209.1 4.3 %reduce_sum.124 = bf16[3,4,64,1152]{3,2,1,0:T(8,128)(2,1)} reduce(bf16[2,3,4,64,1152]{4,3,2,1,0:T(8,128)(2,1)} %bitcast.105, bf16[]{:T(256)} %constant.99.clone.1), dimensions={0}, to_apply=%region_16.17 | reduce | flops 884736 | bytes 5308418 | tf_op jit(solution)/shard_map/reduce_sum | solution.py:224
  213.5 2.2 convert_reduce_fusion.1
  215.7 0.6 fusion.24
  216.3 0.6 copy-done.2
  216.9 2.5 fusion.27
  219.4 60.6 %all-gather.10.cloned.1.call-done = bf16[1152,2304]{1,0:T(8,128)(2,1)} async-done(((bf16[1152,1152]{1,0:T(8,128)(2,1)}), bf16[1152,2304]{1,0:T(8,128)(2,1)}) %all-gather.10.cloned.1.call-update) | async-done | bytes 5308432 | tf_op jit(solution)/shard_map/all_gather | solution.py:234
  280.0 70.7 %all-gather.8.cloned.1.call-done = bf16[1152,2304]{1,0:T(8,128)(2,1)} async-done(((bf16[1152,1152]{1,0:T(8,128)(2,1)}), bf16[1152,2304]{1,0:T(8,128)(2,1)}) %all-gather.8.cloned.1.call-update) | async-done | bytes 5308432 | tf_op jit(solution)/shard_map/all_gather | solution.py:233
  350.7 15.5 %fusion.31 = bf16[768,1152]{1,0:T(8,128)(2,1)} fusion(bf16[1152,2304]{1,0:T(8,128)(2,1)} %all-gather.10.cloned.1.call-done, bf16[768,1152]{1,0:T(8,128)(2,1)} %bitcast.109, bf16[1152,2304]{1,0:T(8,128)(2,1)} %all-gather.8.cloned.1.call-done), kind=kOutput, calls=%fused_computation.41 | convolution fusion | flops 8170536960 | bytes 14155776 | tf_op jit(solution)/shard_map/dot_general | solution.py:238
  366.3 28.5 %reduce-scatter.2.cloned.1.call-done = bf16[3,4,32,1152]{3,2,1,0:T(8,128)(2,1)} async-done(((bf16[3,4,64,1152]{3,2,1,0:T(8,128)(2,1)}), bf16[3,4,32,1152]{3,2,1,0:T(8,128)(2,1)}) %reduce-scatter.2.cloned.1.call-update) | async-done | bytes 884752 | tf_op jit(solution)/shard_map/reduce_scatter | solution.py:241
  394.7 2.6 add_convert_fusion
  (81 shorter events, 2.8 us)
Async XLA Ops:
  6.5 18.5 %copy-start = (bf16[144,6912]{1,0:T(8,128)(2,1)S(1)}, bf16[144,6912]{1,0:T(8,128)(2,1)}, u32[]{:S(2)}) copy-start(bf16[144,6912]{1,0:T(8,128)(2,1)} %param.23) | copy-start | bytes 5971972
  6.5 54.4 %copy-start.11 = (s32[3]{0:T(128)S(1)}, s32[3]{0:T(128)}, u32[]{:S(2)}) copy-start(s32[3]{0:T(128)} %param.16) | copy-start | bytes 40
  6.5 18.5 %copy-start.10 = (s32[3]{0:T(128)S(1)}, s32[3]{0:T(128)}, u32[]{:S(2)}) copy-start(s32[3]{0:T(128)} %param.17) | copy-start | bytes 40
  6.5 18.5 %copy-start.7 = (bf16[1001,144]{0,1:T(8,128)(2,1)S(1)}, bf16[1001,144]{0,1:T(8,128)(2,1)}, u32[]{:S(2)}) copy-start(bf16[1001,144]{0,1:T(8,128)(2,1)} %param.22) | copy-start | bytes 864868
  6.5 97.6 %all-gather.6.cloned.1.call-start = ((), (), s32[]{:S(2)}) async-start(), calls=%async_computation.1 | async-start | bytes 4423680 | tf_op jit(solution)/shard_map/all_gather | solution.py:198
  16.2 0.7 copy-start.4
  17.7 44.7 %collective-permute-start = (f32[3,1,64,4]{3,1,0,2:T(1,128)}, f32[3,1,64,4]{3,1,0,2:T(1,128)S(1)}, u32[]{:S(2)}, u32[]{:S(2)}) collective-permute-start(f32[3,1,64,4]{3,1,0,2:T(1,128)} %get-tuple-element.21), channel_id=1, source_target_pairs={{0,4},{4,8},{8,12},{12,16},{16,20},{20,24},{24,28},{1,5},{5,9},{9,... | collective-permute-start | bytes 9224 | tf_op jit(solution)/shard_map/ppermute | solution.py:16
  19.0 43.4 %collective-permute-start.1 = (f32[3,1,64,4]{3,1,0,2:T(1,128)}, f32[3,1,64,4]{3,1,0,2:T(1,128)S(1)}, u32[]{:S(2)}, u32[]{:S(2)}) collective-permute-start(f32[3,1,64,4]{3,1,0,2:T(1,128)} %get-tuple-element.22), channel_id=1, source_target_pairs={{4,0},{8,4},{12,8},{16,12},{20,16},{24,20},{28,24},{5,1},{9,5},{13... | collective-permute-start | bytes 9224 | tf_op jit(solution)/shard_map/ppermute | solution.py:19
  22.7 186.5 %all-gather.12.cloned.1.call-start = ((), (), s32[]{:S(2)}) async-start(), calls=%async_computation.5 | async-start | bytes 5308416 | tf_op jit(solution)/shard_map/all_gather | solution.py:224
  25.8 36.4 %copy-start.5 = (f32[3,4,64,4]{3,1,0,2:T(4,128)S(1)}, f32[3,4,64,4]{3,1,0,2:T(4,128)}, u32[]{:S(2)}) copy-start(f32[3,4,64,4]{3,1,0,2:T(4,128)} %copy-done.4) | copy-start | bytes 36868
  60.7 2.7 copy-start.8
  78.0 6.5 %copy-start.12 = (bf16[1152,3,576]{0,2,1:T(8,128)(2,1)S(1)}, bf16[1152,3,576]{0,2,1:T(8,128)(2,1)}, u32[]{:S(2)}) copy-start(bf16[1152,3,576]{0,2,1:T(8,128)(2,1)} %param.24) | copy-start | bytes 11943940
  138.4 8.4 %copy-start.3 = (f32[3,8,256,512]{3,2,1,0:T(8,128)S(1)}, f32[3,8,256,512]{3,2,1,0:T(8,128)}, u32[]{:S(2)}) copy-start(f32[3,8,256,512]{3,2,1,0:T(8,128)} %get-tuple-element.52) | copy-start | bytes 37748740
  152.9 4.0 copy-start.6
  161.4 118.6 %all-gather.10.cloned.1.call-start = ((), (), s32[]{:S(2)}) async-start(), calls=%async_computation.3 | async-start | bytes 7962624 | tf_op jit(solution)/shard_map/all_gather | solution.py:234
  162.1 51.3 %copy-start.9 = (f32[3,1152]{1,0:T(4,128)S(1)}, f32[3,1152]{1,0:T(4,128)}, u32[]{:S(2)}) copy-start(f32[3,1152]{1,0:T(4,128)} %get-tuple-element.27) | copy-start | bytes 41476
  162.2 188.6 %all-gather.8.cloned.1.call-start = ((), (), s32[]{:S(2)}) async-start(), calls=%async_computation.2 | async-start | bytes 7962624 | tf_op jit(solution)/shard_map/all_gather | solution.py:233
  162.7 232.0 %reduce-scatter.2.cloned.1.call-start = ((), (), s32[]{:S(2)}) async-start(), calls=%async_computation.4 | async-start | bytes 2654208 | tf_op jit(solution)/shard_map/reduce_scatter | solution.py:241
  215.7 1.2 copy-start.2
  350.7 46.6 %copy-start.1 = (bf16[144,6912]{1,0:T(8,128)(2,1)S(1)}, bf16[144,6912]{1,0:T(8,128)(2,1)}, u32[]{:S(2)}) copy-start(bf16[144,6912]{1,0:T(8,128)(2,1)} %param.23) | copy-start | bytes 5971972
Sparse Core Ops, SparseCore 0:
  22.8 50.2 all-gather.5
  161.5 47.5 all-gather.11
  210.7 69.2 all-gather.9
  281.4 69.2 all-gather.7
  366.4 28.3 reduce-scatter.1
